TPU v7x, 256 devices: a whole 4x4x8 slice. The times are simulated.
256 devices in a mesh: src: 128 (over x, z, y), lev: 2 (over core).
Axes of the slice: x: 4, y: 4, z: 8, core: 2. Of those that a mesh axis runs over, the one named last changes fastest.
Arguments:
- field: bfloat16 [262144, 256], P('src', 'lev'), may hold values from -6 to 6
- grad_coef: float32 [2, 4, 262144], P(None, None, 'src'), may hold values from -6 to 6
- neighbours: int32 [262144, 4], P('src'), may hold values from 0 to 2175, as said below
- level_weight: float32 [8], replicated, may hold values from 0.2 to 2
- src_index: int32 [16384, 64], P('src'), may hold values from 0 to 2047
- tgt_index: int32 [16384, 32], P('src'), may hold values from 0 to 1023
- block_dest: int32 [16384, 1], P('src'), may hold values from 0 to 127; in each aligned block of 128 rows (0 to 127, 128 to 255, ...) at most 2 rows name the same one
- weights: bfloat16 [16384, 6144], P('src'), may hold values from -0.21875 to 0.21875
Outputs:
- remapped: bfloat16 [131072, 256], P('src', 'lev')
- column_total: float32 [32, 131072], P(None, 'src')
Inputs may be any that keep to these rules, and one draw needn't show every extreme that they name: `neighbours`: position 64 + p is the device's own cell p; positions below 64 and from 2112 on are the last and first cells of the devices before and after along the closed curve; a neighbour lies at most 64 cells from the cell. `block_dest`: the 128 blocks of one index of src name one target index at most 2 times.
All inputs are finite; a program needn't handle non-finite values.
Results may differ from a plain program's by a relative error of at most 0.0049.
Values may be sent and summed in bfloat16 or wider, within the bound.
No kernel may reach another device: no remote copies, remote signals or barrier semaphores. Data moves between devices by JAX's collectives and lax.ppermute only.
A program may use at most 128 MiB of HBM per device.

v0:
```python
import jax
import jax.numpy as jnp
from jax import lax
from jax.sharding import PartitionSpec as P

FIELDS = 32
HW = 64
SB = 64
TB = 32
T_DEV = 1024


def extended_2(block, sides, width):
    for axis, dim in sides:
        count = lax.axis_size(axis)
        forward = [(i, i + 1) for i in range(count - 1)]
        forward.append((count - 1, 0))
        backward = [(target, source) for source, target in forward]
        low = lax.ppermute(
            lax.slice_in_dim(block, block.shape[dim] - width, None, axis=dim), axis, forward
        )
        high = lax.ppermute(lax.slice_in_dim(block, 0, width, axis=dim), axis, backward)
        block = jnp.concatenate([low, block, high], axis=dim)
    return block


def block_product(block_weights, block_rows):
    block_count = block_rows.shape[0]
    shaped = block_weights.reshape(block_count, 3 * SB, TB)
    return lax.dot_general(
        shaped, block_rows, (((1,), (1,)), ((0,), (0,))), preferred_element_type=jnp.float32
    )


def shards(field, grad_coef, neighbours, level_weight, src_index, tgt_index, block_dest, weights):
    extended = extended_2(field, (("src", 0),), HW)
    own_float = field.astype(jnp.float32)
    differ = extended[neighbours].astype(jnp.float32) - own_float[:, None, :]
    grad_east = jnp.sum(grad_coef[0].T[:, :, None] * differ, axis=1).astype(jnp.bfloat16)
    grad_north = jnp.sum(grad_coef[1].T[:, :, None] * differ, axis=1).astype(jnp.bfloat16)
    recon = jnp.stack([field, grad_east, grad_north])
    columns = field.shape[1]
    block_count = src_index.shape[0]
    block_rows = jnp.transpose(recon[:, src_index], (1, 0, 2, 3)).reshape(
        block_count, 3 * SB, columns
    )
    src_count = lax.axis_size("src")
    capacity = 2 * block_count // src_count
    target_owner = block_dest[:, 0]
    onehot = (target_owner[:, None] == jnp.arange(src_count, dtype=jnp.int32)[None, :]).astype(
        jnp.int32
    )
    before = jnp.cumsum(onehot, axis=0) - onehot
    slot_rank = jnp.sum(before * onehot, axis=1)
    slot_index = target_owner * capacity + slot_rank
    slots = src_count * capacity
    send_cells = jnp.zeros((slots, TB), jnp.int32).at[slot_index].set(tgt_index)
    recv_cells = lax.all_to_all(send_cells, "src", split_axis=0, concat_axis=0, tiled=True)
    send_rows = jnp.zeros((slots, 3 * SB, columns), jnp.bfloat16).at[slot_index].set(block_rows)
    send_weights = jnp.zeros((slots, weights.shape[1]), jnp.bfloat16).at[slot_index].set(weights)
    got_rows, got_weights = (
        lax.all_to_all(send_rows, "src", split_axis=0, concat_axis=0, tiled=True),
        lax.all_to_all(send_weights, "src", split_axis=0, concat_axis=0, tiled=True),
    )
    received = block_product(got_weights, got_rows)
    total = (
        jnp.zeros((T_DEV, columns), jnp.float32)
        .at[recv_cells.reshape(-1)]
        .add(received.reshape(-1, columns))
    )
    remapped = total.astype(jnp.bfloat16)
    level_count = columns // FIELDS
    level_share = lax.dynamic_slice_in_dim(
        level_weight, lax.axis_index("lev") * level_count, level_count
    )
    local_sum = jnp.einsum(
        "tlf,l->ft",
        total.reshape(T_DEV, level_count, FIELDS),
        level_share,
        precision=lax.Precision.HIGHEST,
    )
    column_total = lax.psum(local_sum, "lev")
    return (remapped, column_total)


def solution(mesh):
    placed = (
        P("src", "lev"),
        P(None, None, "src"),
        P("src", None),
        P(),
        P("src", None),
        P("src", None),
        P("src", None),
        P("src", None),
    )
    return jax.shard_map(
        shards,
        mesh=mesh,
        in_specs=placed,
        out_specs=(P("src", "lev"), P(None, "src")),
        check_vma=False,
    )
```

profile of v0, /device:TPU:1, one launch (start us, length us, event | category | flops | bytes accessed | tf_op | source)
XLA Modules:
  0.0 694.0 jit_solution(10365732698928579888)
XLA Ops:
  7.2 0.0 copy-start
  7.2 0.7 fusion.10
  7.9 0.2 reduce_window_sum.11
  8.1 0.8 select_reduce_fusion
  8.9 0.7 fusion.13
  9.6 0.8 copy.21
  10.4 1.5 scatter_custom_fusion
  11.9 16.3 %all-to-all-start = ((s32[128,2,32]{2,1,0:T(2,128)}), s32[128,2,32]{2,1,0:T(2,128)S(1)}, u32[]{:S(2)}, u32[]{:S(2)}) async-start(s32[128,2,32]{2,1,0:T(2,128)} %bitcast.3), calls=%async_computation | async-start | bytes 262144 | tf_op jit(solution)/shard_map/all_to_all | solution.py:58
  28.2 4.6 scatter_custom_fusion.1
  32.9 3.3 all_to_all.17
  36.2 0.0 copy-start.1
  36.2 0.0 copy-start.4
  36.2 0.0 copy-start.5
  36.2 0.0 copy-start.3
  36.2 3.0 all-to-all-done
  39.2 10.9 %all-to-all-start.1 = ((bf16[128,2,6144]{2,1,0:T(2,128)(2,1)}), bf16[128,2,6144]{2,1,0:T(2,128)(2,1)}, u32[]{:S(2)}, u32[]{:S(2)}) async-start(bf16[128,2,6144]{2,1,0:T(2,128)(2,1)} %all_to_all.17), calls=%async_computation.1 | async-start | bytes 6291456 | tf_op jit(solution)/shard_map/all_to_all | solution.py:63
  50.1 0.0 copy-done.1
  50.1 0.6 collective-permute-start
  50.7 6.8 collective-permute-start.1
  57.5 0.0 copy-done.4
  57.5 0.4 copy.23
  57.9 0.6 reshape.80
  58.6 0.0 copy-done.5
  58.6 0.1 copy.28
  58.7 0.1 reshape.88
  58.8 0.0 copy-done.3
  58.8 1.1 convert_element_type.40
  59.9 1.4 copy.22
  61.3 1.4 copy.24
  62.6 8.9 %copy.25 = bf16[1,2048,128]{2,0,1:T(2,128)(2,1)} copy(bf16[1,2048,128]{2,1,0:T(8,128)(2,1)S(1)} %bitcast.44) | data formatting | bytes 1048576 | tf_op jit(solution)/shard_map/stack | solution.py:41
  71.5 49.4 %collective-permute-done = bf16[64,128]{1,0:T(8,128)(2,1)S(1)} collective-permute-done((bf16[64,128]{1,0:T(8,128)(2,1)S(1)}, bf16[64,128]{1,0:T(8,128)(2,1)S(1)}, u32[]{:S(2)}, u32[]{:S(2)}) %collective-permute-start) | collective-permute-done | bytes 16416 | tf_op jit(solution)/shard_map/ppermute | solution.py:19
  121.0 0.0 collective-permute-done.1
  121.0 24.0 %gather_fusion = bf16[8192,128]{1,0:T(8,128)(2,1)S(1)} fusion(bf16[2176,128]{1,0:T(8,128)(2,1)S(1)} %pad_maximum_fusion.1, s32[8192]{0:T(1024)S(1)} %broadcast_clamp_fusion.1), kind=kCustom, calls=%fused_computation | custom fusion | bytes 4227072 | tf_op jit(solution)/shard_map/gather | solution.py:38
  145.1 0.0 copy-start.2
  145.1 15.1 %fusion.2 = (bf16[2048,128]{1,0:T(8,128)(2,1)S(1)}, bf16[2048,128]{1,0:T(8,128)(2,1)S(1)}) fusion(bf16[2048,4,128]{2,1,0:T(4,128)(2,1)S(1)} %bitcast.43, f32[2048,128]{1,0:T(8,128)} %convert_element_type.40, f32[2048,4]{1,0:T(8,128)} %copy.22, f32[2048,4]{1,0:T(8,128)} %copy.24), kind=kLoop, calls=%fused_computation.9 | loop fusion | flops 5767168 | bytes 4259840 | tf_op jit(solution)/shard_map/reduce_sum | solution.py:39
  160.1 8.1 %copy.26 = bf16[1,2048,128]{2,0,1:T(2,128)(2,1)S(1)} copy(bf16[1,2048,128]{2,1,0:T(8,128)(2,1)S(1)} %bitcast.47) | data formatting | bytes 1048576 | tf_op jit(solution)/shard_map/convert_element_type | solution.py:39
  168.3 8.3 %copy.27 = bf16[1,2048,128]{2,0,1:T(2,128)(2,1)S(1)} copy(bf16[1,2048,128]{2,1,0:T(8,128)(2,1)S(1)} %bitcast.46) | data formatting | bytes 1048576 | tf_op jit(solution)/shard_map/convert_element_type | solution.py:40
  176.6 0.0 copy-done.2
  176.6 3.6 pad_maximum_fusion
  180.2 56.5 %gather_fusion.1 = bf16[8192,3,128]{2,1,0:T(4,128)(2,1)} fusion(bf16[3,2048,128]{2,0,1:T(4,128)(2,1)S(1)} %pad_maximum_fusion, s32[8192]{0:T(1024)S(1)} %broadcast_clamp_fusion), kind=kCustom, calls=%fused_computation.1 | custom fusion | bytes 12615680 | tf_op jit(solution)/shard_map/gather | solution.py:44
  236.6 8.0 %copy.29 = bf16[128,64,3,128]{3,1,2,0:T(8,128)(2,1)} copy(bf16[128,64,3,128]{3,2,1,0:T(4,128)(2,1)} %bitcast.40) | data formatting | bytes 12582912 | tf_op jit(solution)/shard_map/gather | solution.py:44
  244.7 7.8 %broadcast_in_dim.29 = bf16[256,192,128]{2,1,0:T(8,128)(2,1)} broadcast(bf16[]{:T(256)} %constant.16.clone.1), dimensions={} | broadcast | bytes 12582914 | tf_op jit(solution)/shard_map/broadcast_in_dim | solution.py:59
  252.4 21.5 %scatter_fusion = bf16[256,192,128]{2,1,0:T(8,128)(2,1)} fusion(bf16[256,192,128]{2,1,0:T(8,128)(2,1)} %broadcast_in_dim.29, s32[128]{0:T(128)S(1)} %fusion.13, bf16[128,192,128]{2,1,0:T(8,128)(2,1)} %bitcast.41), kind=kCustom, calls=%fused_computation.4 | custom fusion | bytes 18874880 | tf_op jit(solution)/shard_map/scatter | solution.py:59
  274.0 0.0 all-to-all-done.1
  274.0 9.4 %all-to-all-start.2 = ((bf16[256,192,128]{2,1,0:T(8,128)(2,1)}), bf16[256,192,128]{2,1,0:T(8,128)(2,1)}, u32[]{:S(2)}, u32[]{:S(2)}) async-start(bf16[256,192,128]{2,1,0:T(8,128)(2,1)} %scatter_fusion), calls=%async_computation.2 | async-start | bytes 25165824 | tf_op jit(solution)/shard_map/all_to_all | solution.py:62
  283.3 0.0 all-reduce.2.cloned.1.call-start
  283.4 0.2 reshape.73
  283.6 16.2 %reshape.74 = bf16[256,192,32]{2,1,0:T(8,128)(2,1)} reshape(bf16[128,2,6144]{2,1,0:T(2,128)(2,1)} %all-to-all-done.1) | data formatting | bytes 6291456 | tf_op jit(solution)/shard_map/reshape | solution.py:29
  299.8 254.6 %all-to-all-done.2 = bf16[256,192,128]{2,1,0:T(8,128)(2,1)} async-done(((bf16[256,192,128]{2,1,0:T(8,128)(2,1)}), bf16[256,192,128]{2,1,0:T(8,128)(2,1)}, u32[]{:S(2)}, u32[]{:S(2)}) %all-to-all-start.2) | async-done | bytes 12582944 | tf_op jit(solution)/shard_map/all_to_all | solution.py:62
  554.4 12.1 %fusion.17 = f32[256,32,128]{2,1,0:T(8,128)} fusion(bf16[256,192,32]{2,1,0:T(8,128)(2,1)} %reshape.74, bf16[256,192,128]{2,1,0:T(8,128)(2,1)} %all-to-all-done.2), kind=kOutput, calls=%fused_computation.39 | convolution fusion | flops 402653184 | bytes 19922944 | tf_op jit(solution)/shard_map/dot_general | solution.py:30
  566.4 44.4 %scatter_custom_fusion.3 = f32[1024,128]{1,0:T(8,128)S(1)} fusion(s32[8192]{0:T(1024)S(1)} %bitcast.49, f32[8192,128]{1,0:T(8,128)} %bitcast.42, f32[]{:T(128)} %constant.11.clone.1), kind=kCustom, calls=%fused_computation.19 | custom fusion | flops 1048576 | bytes 524800 | tf_op jit(solution)/shard_map/scatter-add | solution.py:69
  610.9 0.2 copy.31
  611.1 0.0 copy-done
  611.1 28.9 %fusion.6 = f32[1,1024,32]{0,1,2:T(8,128)} fusion(f32[1024,4,32]{0,2,1:T(8,128)S(1)} %bitcast.45, f32[8]{0:T(128)S(1)} %copy-done, s32[]{:T(128)S(6)} %select_n.29), kind=kOutput, calls=%fused_computation.15 | convolution fusion | flops 1572864 | bytes 655396 | tf_op jit(solution)/shard_map/tlf,l->ft/dot_general | solution.py:76
  640.0 10.6 %copy.34 = f32[1,1024,32]{1,2,0:T(8,128)} copy(f32[1,1024,32]{0,1,2:T(8,128)} %fusion.6) | data formatting | bytes 262144 | tf_op jit(solution)/shard_map/tlf,l->ft/dot_general | solution.py:76
  650.5 0.0 all-reduce.2.cloned.1.call-update
  650.6 0.7 convert_element_type.45
  651.3 34.0 %all-reduce.2.cloned.1.call-done = f32[32,1024]{1,0:T(8,128)} async-done(((f32[32,1024]{1,0:T(8,128)}), f32[32,1024]{1,0:T(8,128)}) %all-reduce.2.cloned.1.call-update) | async-done | bytes 131088 | tf_op jit(solution)/shard_map/psum | solution.py:82
  685.3 1.6 copy.39
  (8 shorter events, 0.1 us)
Async XLA Ops:
  7.2 603.9 %copy-start = (f32[8]{0:T(128)S(1)}, f32[8]{0:T(128)}, u32[]{:S(2)}) copy-start(f32[8]{0:T(128)} %param.11) | copy-start | bytes 100
  11.9 27.3 %all-to-all-start = ((s32[128,2,32]{2,1,0:T(2,128)}), s32[128,2,32]{2,1,0:T(2,128)S(1)}, u32[]{:S(2)}, u32[]{:S(2)}) async-start(s32[128,2,32]{2,1,0:T(2,128)} %bitcast.3), calls=%async_computation | async-start | bytes 262144 | tf_op jit(solution)/shard_map/all_to_all | solution.py:58
  36.2 13.9 %copy-start.1 = (bf16[2048,128]{1,0:T(8,128)(2,1)S(1)}, bf16[2048,128]{1,0:T(8,128)(2,1)}, u32[]{:S(2)}) copy-start(bf16[2048,128]{1,0:T(8,128)(2,1)} %param.8) | copy-start | bytes 1572868
  36.2 21.3 %copy-start.4 = (s32[2048,4]{0,1:T(4,128)S(1)}, s32[2048,4]{0,1:T(4,128)}, u32[]{:S(2)}) copy-start(s32[2048,4]{0,1:T(4,128)} %param.10) | copy-start | bytes 98308
  36.2 22.3 %copy-start.5 = (s32[128,64]{0,1:T(8,128)S(1)}, s32[128,64]{0,1:T(8,128)}, u32[]{:S(2)}) copy-start(s32[128,64]{0,1:T(8,128)} %param.12) | copy-start | bytes 98308
  36.2 22.5 %copy-start.3 = (f32[2,4,2048]{2,1,0:T(4,128)S(1)}, f32[2,4,2048]{2,1,0:T(4,128)}, u32[]{:S(2)}) copy-start(f32[2,4,2048]{2,1,0:T(4,128)} %param.9) | copy-start | bytes 196612
  39.2 234.8 %all-to-all-start.1 = ((bf16[128,2,6144]{2,1,0:T(2,128)(2,1)}), bf16[128,2,6144]{2,1,0:T(2,128)(2,1)}, u32[]{:S(2)}, u32[]{:S(2)}) async-start(bf16[128,2,6144]{2,1,0:T(2,128)(2,1)} %all_to_all.17), calls=%async_computation.1 | async-start | bytes 6291456 | tf_op jit(solution)/shard_map/all_to_all | solution.py:63
  50.1 70.9 %collective-permute-start = (bf16[64,128]{1,0:T(8,128)(2,1)S(1)}, bf16[64,128]{1,0:T(8,128)(2,1)S(1)}, u32[]{:S(2)}, u32[]{:S(2)}) collective-permute-start(bf16[64,128]{1,0:T(8,128)(2,1)S(1)} %get-tuple-element.4), channel_id=1, source_target_pairs={{0,2},{2,4},{4,6},{6,8},{8,10},{10,12},{12,14},{14,16},{16,18},{18... | collective-permute-start | bytes 49160 | tf_op jit(solution)/shard_map/ppermute | solution.py:19
  50.7 70.3 %collective-permute-start.1 = (bf16[64,128]{1,0:T(8,128)(2,1)S(1)}, bf16[64,128]{1,0:T(8,128)(2,1)S(1)}, u32[]{:S(2)}, u32[]{:S(2)}) collective-permute-start(bf16[64,128]{1,0:T(8,128)(2,1)S(1)} %get-tuple-element.5), channel_id=1, source_target_pairs={{2,0},{4,2},{6,4},{8,6},{10,8},{12,10},{14,12},{16,14},{18,16},{20... | collective-permute-start | bytes 49160 | tf_op jit(solution)/shard_map/ppermute | solution.py:22
  145.1 31.5 %copy-start.2 = (bf16[1,2048,128]{2,0,1:T(2,128)(2,1)S(1)}, bf16[1,2048,128]{2,0,1:T(2,128)(2,1)}, u32[]{:S(2)}) copy-start(bf16[1,2048,128]{2,0,1:T(2,128)(2,1)} %copy.25) | copy-start | bytes 1572868
  274.0 280.4 %all-to-all-start.2 = ((bf16[256,192,128]{2,1,0:T(8,128)(2,1)}), bf16[256,192,128]{2,1,0:T(8,128)(2,1)}, u32[]{:S(2)}, u32[]{:S(2)}) async-start(bf16[256,192,128]{2,1,0:T(8,128)(2,1)} %scatter_fusion), calls=%async_computation.2 | async-start | bytes 25165824 | tf_op jit(solution)/shard_map/all_to_all | solution.py:62
  283.3 402.0 %all-reduce.2.cloned.1.call-start = ((), (), s32[]{:S(2)}) async-start(), calls=%async_computation.3 | async-start | bytes 262144 | tf_op jit(solution)/shard_map/psum | solution.py:82
Sparse Core Ops, SparseCore 0:
  650.7 34.5 all-reduce.1
where the time goes:
time: 702 us; the launch traced here: 694 us
  waiting for transfers between devices  341 us (49%)
  local copies, waits for them, and re-layouts  186 us (26%)
  other arithmetic  67.4 us (10%)
  starting transfers between devices  44 us (6%)
  matrix products  40.9 us (6%)
  between operations  14.5 us (2%)
    all_to_all x1, waiting for transfers between devices, shards(): lax.all_to_all(send_rows, 'src', split_axis=0, concat_axis=0, tiled=True)  255 us
    gather x2, local copies, waits for them, and re-layouts, shards(): recon[:, src_index]  64.5 us
    ppermute x1, waiting for transfers between devices, extended_2(): lax.ppermute(lax.slice_in_dim(block, block.shape[dim] - width, None, axis...  49.4 us
    scatter-add x1, other arithmetic, shards(): total = jnp.zeros((T_DEV, columns), jnp.float32).at[recv_cells.reshape(-1...  44.4 us
    psum x1, waiting for transfers between devices, shards(): column_total = lax.psum(local_sum, 'lev')  34 us
    dot_general x1, matrix products, shards(): jnp.einsum('tlf,l->ft', total.reshape(T_DEV, level_count, FIELDS), level_...  28.9 us
    gather x1, local copies, waits for them, and re-layouts, shards(): differ = extended[neighbours].astype(jnp.float32) - own_float[:, None, :]  24 us
    scatter x1, local copies, waits for them, and re-layouts, shards(): jnp.zeros((slots, 3 * SB, columns), jnp.bfloat16).at[slot_index]  21.5 us
  transfers between devices with their start and end apart: 6, of which 4 were waited for; matrix products, arithmetic and copies ran while one was open for 27% of the time, Pallas kernels for 0%

commit v1 on v0

--- a/solution.py
+++ b/solution.py
@@ -8,6 +8,12 @@
 SB = 64
 TB = 32
 T_DEV = 1024
+
+
+def enter_the_task(vector):
+    z2 = lax.all_gather(vector, "lev")
+    x_now = jnp.sum(z2, axis=0)
+    return x_now
 
 
 def extended_2(block, sides, width):
@@ -79,7 +85,7 @@
         level_share,
         precision=lax.Precision.HIGHEST,
     )
-    column_total = lax.psum(local_sum, "lev")
+    column_total = enter_the_task(local_sum)
     return (remapped, column_total)
 
 

time: 702 us -> 665 us (0.947)
  waiting for transfers between devices: 341 us -> 308 us
  between operations: 14.5 us -> 1.09 us
  blocking collectives: 0 us -> 7.46 us
    psum x1 -> x0, waiting for transfers between devices: 34 us -> none  [shards(): column_total = lax.psum(local_sum, 'lev')]
    all_gather x0 -> x1, blocking collectives: none -> 7.46 us  [enter_the_task(): z2 = lax.all_gather(vector, 'lev')]
  transfers between devices with their start and end apart: 6 -> 5, of which waited for: 4 -> 3; matrix products, arithmetic and copies ran while one was open for 27% -> 29% of each run, Pallas kernels for 0% -> 0%
where the time goes in v1:
time: 665 us; the launch traced here: 654 us
  waiting for transfers between devices  308 us (46%)
  local copies, waits for them, and re-layouts  184 us (28%)
  other arithmetic  68 us (10%)
  starting transfers between devices  44.2 us (7%)
  matrix products  40.9 us (6%)
  blocking collectives  7.46 us (1%)
    all_to_all x1, waiting for transfers between devices, shards(): lax.all_to_all(send_rows, 'src', split_axis=0, concat_axis=0, tiled=True)  256 us
    gather x2, local copies, waits for them, and re-layouts, shards(): recon[:, src_index]  64.5 us
    ppermute x1, waiting for transfers between devices, extended_2(): lax.ppermute(lax.slice_in_dim(block, block.shape[dim] - width, None, axis...  49.4 us
    scatter-add x1, other arithmetic, shards(): total = jnp.zeros((T_DEV, columns), jnp.float32).at[recv_cells.reshape(-1...  44.4 us
    dot_general x1, matrix products, shards(): jnp.einsum('tlf,l->ft', total.reshape(T_DEV, level_count, FIELDS), level_...  28.9 us
    gather x1, local copies, waits for them, and re-layouts, shards(): differ = extended[neighbours].astype(jnp.float32) - own_float[:, None, :]  24 us
    scatter x1, local copies, waits for them, and re-layouts, shards(): jnp.zeros((slots, 3 * SB, columns), jnp.bfloat16).at[slot_index]  21.5 us
    all_to_all x1, starting transfers between devices, shards(): lax.all_to_all(send_cells, 'src', split_axis=0, concat_axis=0, tiled=True)  16.3 us
  transfers between devices with their start and end apart: 5, of which 3 were waited for; matrix products, arithmetic and copies ran while one was open for 29% of the time, Pallas kernels for 0%

profile of v1, /device:TPU:1, one launch (start us, length us, event | category | flops | bytes accessed | tf_op | source)
XLA Modules:
  0.0 653.9 jit_solution(9968357007114933240)
XLA Ops:
  0.6 0.0 copy-start
  0.6 0.7 fusion.10
  1.4 0.2 reduce_window_sum.11
  1.6 0.8 select_reduce_fusion
  2.4 0.7 fusion.13
  3.1 0.8 copy.21
  3.9 1.5 scatter_custom_fusion
  5.4 16.3 %all-to-all-start = ((s32[128,2,32]{2,1,0:T(2,128)}), s32[128,2,32]{2,1,0:T(2,128)S(1)}, u32[]{:S(2)}, u32[]{:S(2)}) async-start(s32[128,2,32]{2,1,0:T(2,128)} %bitcast.3), calls=%async_computation | async-start | bytes 262144 | tf_op jit(solution)/shard_map/all_to_all | solution.py:64
  21.7 4.6 scatter_custom_fusion.1
  26.3 3.3 all_to_all.17
  29.7 0.0 copy-start.1
  29.7 0.0 copy-start.4
  29.7 0.0 copy-start.5
  29.7 0.0 copy-start.3
  29.7 3.0 all-to-all-done
  32.7 10.9 %all-to-all-start.1 = ((bf16[128,2,6144]{2,1,0:T(2,128)(2,1)}), bf16[128,2,6144]{2,1,0:T(2,128)(2,1)}, u32[]{:S(2)}, u32[]{:S(2)}) async-start(bf16[128,2,6144]{2,1,0:T(2,128)(2,1)} %all_to_all.17), calls=%async_computation.1 | async-start | bytes 6291456 | tf_op jit(solution)/shard_map/all_to_all | solution.py:69
  43.6 0.0 copy-done.1
  43.6 0.6 collective-permute-start
  44.2 6.8 %collective-permute-start.1 = (bf16[64,128]{1,0:T(8,128)(2,1)S(1)}, bf16[64,128]{1,0:T(8,128)(2,1)S(1)}, u32[]{:S(2)}, u32[]{:S(2)}) collective-permute-start(bf16[64,128]{1,0:T(8,128)(2,1)S(1)} %get-tuple-element.5), channel_id=1, source_target_pairs={{2,0},{4,2},{6,4},{8,6},{10,8},{12,10},{14,12},{16,14},{18,16},{20... | collective-permute-start | bytes 49160 | tf_op jit(solution)/shard_map/ppermute | solution.py:28
  51.0 0.0 copy-done.4
  51.0 0.4 copy.23
  51.4 0.6 reshape.80
  52.0 0.0 copy-done.5
  52.0 0.1 copy.28
  52.1 0.1 reshape.88
  52.2 0.0 copy-done.3
  52.3 1.1 convert_element_type.40
  53.3 1.4 copy.22
  54.7 1.4 copy.24
  56.1 8.9 %copy.25 = bf16[1,2048,128]{2,0,1:T(2,128)(2,1)} copy(bf16[1,2048,128]{2,1,0:T(8,128)(2,1)S(1)} %bitcast.45) | data formatting | bytes 1048576 | tf_op jit(solution)/shard_map/stack | solution.py:47
  65.0 49.4 %collective-permute-done = bf16[64,128]{1,0:T(8,128)(2,1)S(1)} collective-permute-done((bf16[64,128]{1,0:T(8,128)(2,1)S(1)}, bf16[64,128]{1,0:T(8,128)(2,1)S(1)}, u32[]{:S(2)}, u32[]{:S(2)}) %collective-permute-start) | collective-permute-done | bytes 16416 | tf_op jit(solution)/shard_map/ppermute | solution.py:25
  114.4 0.0 collective-permute-done.1
  114.5 24.0 %gather_fusion = bf16[8192,128]{1,0:T(8,128)(2,1)S(1)} fusion(bf16[2176,128]{1,0:T(8,128)(2,1)S(1)} %pad_maximum_fusion.1, s32[8192]{0:T(1024)S(1)} %broadcast_clamp_fusion.1), kind=kCustom, calls=%fused_computation | custom fusion | bytes 4227072 | tf_op jit(solution)/shard_map/gather | solution.py:44
  138.5 0.0 copy-start.2
  138.5 15.1 %fusion.2 = (bf16[2048,128]{1,0:T(8,128)(2,1)S(1)}, bf16[2048,128]{1,0:T(8,128)(2,1)S(1)}) fusion(bf16[2048,4,128]{2,1,0:T(4,128)(2,1)S(1)} %bitcast.44, f32[2048,128]{1,0:T(8,128)} %convert_element_type.40, f32[2048,4]{1,0:T(8,128)} %copy.22, f32[2048,4]{1,0:T(8,128)} %copy.24), kind=kLoop, calls=%fused_computation.9 | loop fusion | flops 5767168 | bytes 4259840 | tf_op jit(solution)/shard_map/reduce_sum | solution.py:45
  153.6 8.1 %copy.26 = bf16[1,2048,128]{2,0,1:T(2,128)(2,1)S(1)} copy(bf16[1,2048,128]{2,1,0:T(8,128)(2,1)S(1)} %bitcast.48) | data formatting | bytes 1048576 | tf_op jit(solution)/shard_map/convert_element_type | solution.py:45
  161.7 8.3 %copy.27 = bf16[1,2048,128]{2,0,1:T(2,128)(2,1)S(1)} copy(bf16[1,2048,128]{2,1,0:T(8,128)(2,1)S(1)} %bitcast.47) | data formatting | bytes 1048576 | tf_op jit(solution)/shard_map/convert_element_type | solution.py:46
  170.1 0.0 copy-done.2
  170.1 3.6 pad_maximum_fusion
  173.6 56.5 %gather_fusion.1 = bf16[8192,3,128]{2,1,0:T(4,128)(2,1)} fusion(bf16[3,2048,128]{2,0,1:T(4,128)(2,1)S(1)} %pad_maximum_fusion, s32[8192]{0:T(1024)S(1)} %broadcast_clamp_fusion), kind=kCustom, calls=%fused_computation.1 | custom fusion | bytes 12615680 | tf_op jit(solution)/shard_map/gather | solution.py:50
  230.1 8.0 %copy.29 = bf16[128,64,3,128]{3,1,2,0:T(8,128)(2,1)} copy(bf16[128,64,3,128]{3,2,1,0:T(4,128)(2,1)} %bitcast.41) | data formatting | bytes 12582912 | tf_op jit(solution)/shard_map/gather | solution.py:50
  238.1 7.8 %broadcast_in_dim.29 = bf16[256,192,128]{2,1,0:T(8,128)(2,1)} broadcast(bf16[]{:T(256)} %constant.16.clone.1), dimensions={} | broadcast | bytes 12582914 | tf_op jit(solution)/shard_map/broadcast_in_dim | solution.py:65
  245.9 21.5 %scatter_fusion = bf16[256,192,128]{2,1,0:T(8,128)(2,1)} fusion(bf16[256,192,128]{2,1,0:T(8,128)(2,1)} %broadcast_in_dim.29, s32[128]{0:T(128)S(1)} %fusion.13, bf16[128,192,128]{2,1,0:T(8,128)(2,1)} %bitcast.42), kind=kCustom, calls=%fused_computation.4 | custom fusion | bytes 18874880 | tf_op jit(solution)/shard_map/scatter | solution.py:65
  267.4 0.0 all-to-all-done.1
  267.4 9.6 %all-to-all-start.2 = ((bf16[256,192,128]{2,1,0:T(8,128)(2,1)}), bf16[256,192,128]{2,1,0:T(8,128)(2,1)}, u32[]{:S(2)}, u32[]{:S(2)}) async-start(bf16[256,192,128]{2,1,0:T(8,128)(2,1)} %scatter_fusion), calls=%async_computation.2 | async-start | bytes 25165824 | tf_op jit(solution)/shard_map/all_to_all | solution.py:68
  277.0 0.2 reshape.73
  277.2 16.0 %reshape.74 = bf16[256,192,32]{2,1,0:T(8,128)(2,1)} reshape(bf16[128,2,6144]{2,1,0:T(2,128)(2,1)} %all-to-all-done.1) | data formatting | bytes 6291456 | tf_op jit(solution)/shard_map/reshape | solution.py:35
  293.2 256.1 %all-to-all-done.2 = bf16[256,192,128]{2,1,0:T(8,128)(2,1)} async-done(((bf16[256,192,128]{2,1,0:T(8,128)(2,1)}), bf16[256,192,128]{2,1,0:T(8,128)(2,1)}, u32[]{:S(2)}, u32[]{:S(2)}) %all-to-all-start.2) | async-done | bytes 12582944 | tf_op jit(solution)/shard_map/all_to_all | solution.py:68
  549.3 12.1 %fusion.17 = f32[256,32,128]{2,1,0:T(8,128)} fusion(bf16[256,192,32]{2,1,0:T(8,128)(2,1)} %reshape.74, bf16[256,192,128]{2,1,0:T(8,128)(2,1)} %all-to-all-done.2), kind=kOutput, calls=%fused_computation.39 | convolution fusion | flops 402653184 | bytes 19922944 | tf_op jit(solution)/shard_map/dot_general | solution.py:36
  561.3 44.4 %scatter_custom_fusion.3 = f32[1024,128]{1,0:T(8,128)S(1)} fusion(s32[8192]{0:T(1024)S(1)} %bitcast.51, f32[8192,128]{1,0:T(8,128)} %bitcast.43, f32[]{:T(128)} %constant.11.clone.1), kind=kCustom, calls=%fused_computation.19 | custom fusion | flops 1048576 | bytes 524800 | tf_op jit(solution)/shard_map/scatter-add | solution.py:75
  605.8 0.2 copy.31
  606.0 0.7 convert_element_type.45
  606.7 0.0 copy-done
  606.7 28.9 %fusion.6 = f32[1,1024,32]{0,1,2:T(8,128)} fusion(f32[1024,4,32]{0,2,1:T(8,128)S(1)} %bitcast.46, f32[8]{0:T(128)S(1)} %copy-done, s32[]{:T(128)S(6)} %select_n.29), kind=kOutput, calls=%fused_computation.15 | convolution fusion | flops 1572864 | bytes 655396 | tf_op jit(solution)/shard_map/tlf,l->ft/dot_general | solution.py:82
  635.6 10.0 %copy.34 = f32[1,1024,32]{1,2,0:T(8,128)S(1)} copy(f32[1,1024,32]{0,1,2:T(8,128)} %fusion.6) | data formatting | bytes 262144 | tf_op jit(solution)/shard_map/tlf,l->ft/dot_general | solution.py:82
  645.5 7.5 %all-gather = f32[64,1024]{1,0:T(8,128)S(1)} all-gather(f32[32,1024]{1,0:T(8,128)S(1)} %bitcast.50), channel_id=2, replica_groups=mesh['src'=128,'lev'=2] {'lev'}, dimensions={0}, use_global_device_ids=true | all-gather | bytes 393216 | tf_op jit(solution)/shard_map/all_gather | solution.py:14
  653.0 0.7 reduce_sum.42
  (8 shorter events, 0.1 us)
Async XLA Ops:
  0.6 606.1 %copy-start = (f32[8]{0:T(128)S(1)}, f32[8]{0:T(128)}, u32[]{:S(2)}) copy-start(f32[8]{0:T(128)} %param.11) | copy-start | bytes 100
  5.4 27.3 %all-to-all-start = ((s32[128,2,32]{2,1,0:T(2,128)}), s32[128,2,32]{2,1,0:T(2,128)S(1)}, u32[]{:S(2)}, u32[]{:S(2)}) async-start(s32[128,2,32]{2,1,0:T(2,128)} %bitcast.3), calls=%async_computation | async-start | bytes 262144 | tf_op jit(solution)/shard_map/all_to_all | solution.py:64
  29.7 13.9 %copy-start.1 = (bf16[2048,128]{1,0:T(8,128)(2,1)S(1)}, bf16[2048,128]{1,0:T(8,128)(2,1)}, u32[]{:S(2)}) copy-start(bf16[2048,128]{1,0:T(8,128)(2,1)} %param.8) | copy-start | bytes 1572868
  29.7 21.3 %copy-start.4 = (s32[2048,4]{0,1:T(4,128)S(1)}, s32[2048,4]{0,1:T(4,128)}, u32[]{:S(2)}) copy-start(s32[2048,4]{0,1:T(4,128)} %param.10) | copy-start | bytes 98308
  29.7 22.3 %copy-start.5 = (s32[128,64]{0,1:T(8,128)S(1)}, s32[128,64]{0,1:T(8,128)}, u32[]{:S(2)}) copy-start(s32[128,64]{0,1:T(8,128)} %param.12) | copy-start | bytes 98308
  29.7 22.5 %copy-start.3 = (f32[2,4,2048]{2,1,0:T(4,128)S(1)}, f32[2,4,2048]{2,1,0:T(4,128)}, u32[]{:S(2)}) copy-start(f32[2,4,2048]{2,1,0:T(4,128)} %param.9) | copy-start | bytes 196612
  32.7 234.8 %all-to-all-start.1 = ((bf16[128,2,6144]{2,1,0:T(2,128)(2,1)}), bf16[128,2,6144]{2,1,0:T(2,128)(2,1)}, u32[]{:S(2)}, u32[]{:S(2)}) async-start(bf16[128,2,6144]{2,1,0:T(2,128)(2,1)} %all_to_all.17), calls=%async_computation.1 | async-start | bytes 6291456 | tf_op jit(solution)/shard_map/all_to_all | solution.py:69
  43.6 70.9 %collective-permute-start = (bf16[64,128]{1,0:T(8,128)(2,1)S(1)}, bf16[64,128]{1,0:T(8,128)(2,1)S(1)}, u32[]{:S(2)}, u32[]{:S(2)}) collective-permute-start(bf16[64,128]{1,0:T(8,128)(2,1)S(1)} %get-tuple-element.4), channel_id=1, source_target_pairs={{0,2},{2,4},{4,6},{6,8},{8,10},{10,12},{12,14},{14,16},{16,18},{18... | collective-permute-start | bytes 49160 | tf_op jit(solution)/shard_map/ppermute | solution.py:25
  44.2 70.3 %collective-permute-start.1 = (bf16[64,128]{1,0:T(8,128)(2,1)S(1)}, bf16[64,128]{1,0:T(8,128)(2,1)S(1)}, u32[]{:S(2)}, u32[]{:S(2)}) collective-permute-start(bf16[64,128]{1,0:T(8,128)(2,1)S(1)} %get-tuple-element.5), channel_id=1, source_target_pairs={{2,0},{4,2},{6,4},{8,6},{10,8},{12,10},{14,12},{16,14},{18,16},{20... | collective-permute-start | bytes 49160 | tf_op jit(solution)/shard_map/ppermute | solution.py:28
  138.5 31.5 %copy-start.2 = (bf16[1,2048,128]{2,0,1:T(2,128)(2,1)S(1)}, bf16[1,2048,128]{2,0,1:T(2,128)(2,1)}, u32[]{:S(2)}) copy-start(bf16[1,2048,128]{2,0,1:T(2,128)(2,1)} %copy.25) | copy-start | bytes 1572868
  267.4 281.9 %all-to-all-start.2 = ((bf16[256,192,128]{2,1,0:T(8,128)(2,1)}), bf16[256,192,128]{2,1,0:T(8,128)(2,1)}, u32[]{:S(2)}, u32[]{:S(2)}) async-start(bf16[256,192,128]{2,1,0:T(8,128)(2,1)} %scatter_fusion), calls=%async_computation.2 | async-start | bytes 25165824 | tf_op jit(solution)/shard_map/all_to_all | solution.py:68
